TPU v7x, 256 devices: a whole 4x4x8 slice. The times are simulated.
256 devices in a mesh: dp: 64 (over x, y, z_lo, core), tensor: 4 (over z_hi).
Axes of the slice: x: 4, y: 4, z: 8 (z_hi: 4, z_lo: 2; z = z_hi * 2 + z_lo), core: 2. Of those that a mesh axis runs over, the one named last changes fastest.
Arguments:
- activations: bfloat16 [49152, 8192], P('dp'), may hold values from -48 to 48
- cotangent: bfloat16 [49152, 1024], P('dp', 'tensor'), may hold values from -0.375 to 0.375
- sampled_rows: int32 [4096], P('dp'), may hold values from 0 to 767
- block_owner: int32 [32], replicated, may hold values from 0 to 63, as said below
Outputs:
- natural_step: float32 [8192, 1024], P('dp', 'tensor')
- owner_block_inverses: float32 [64, 256, 256], P('dp')
Inputs may be any that keep to these rules, and one draw needn't show every extreme that they name: `block_owner`: each index of dp owns either no block or exactly 1 block; block 0 is owned by index 32.
All inputs are finite; a program needn't handle non-finite values. Where the computation divides by a largest or mean magnitude, that divisor is 1e-20 or more.
Results may differ from a plain program's by a relative error of at most 0.0003.
Values may be sent and summed in bfloat16 or wider, within the bound.
A program may use at most 128 MiB of HBM per device.

v0:
```python
import jax
import jax.numpy as jnp
from jax import lax
from jax.sharding import PartitionSpec as P

S_DEV = 64
FACTOR_BLOCK = 256
ITERS = 10
DAMPING = 0.05
precise_mode = lax.Precision.HIGHEST


def from_partner(block, axis, apart):
    count = lax.axis_size(axis)
    route = []
    for low in range(count):
        high = low | 1 << apart
        if high != low and high < count:
            route += [(low, high), (high, low)]
    return lax.ppermute(block, axis, route)


def newton_inverse(matrix):
    extent = matrix.shape[-1]
    identity = jnp.eye(extent, dtype=jnp.float32)
    row_bound = jnp.max(jnp.sum(jnp.abs(matrix), axis=2), axis=1)
    initial = identity[None, :, :] / row_bound[:, None, None]

    def advance(turn_index, current):
        product = jnp.einsum("nij,njk->nik", matrix, current, precision=precise_mode)
        return jnp.einsum(
            "nij,njk->nik", current, 2.0 * identity[None, :, :] - product, precision=precise_mode
        )

    return lax.fori_loop(0, ITERS, advance, initial)


def block_rank(block_owner):
    block_total = block_owner.shape[0]
    same_owner = block_owner[:, None] == block_owner[None, :]
    positions = jnp.arange(block_total, dtype=jnp.int32)
    before = positions[None, :] < positions[:, None]
    return jnp.sum((same_owner & before).astype(jnp.int32), axis=1)


def owner_grams(received):
    return jnp.einsum("pcsk,pcsl->ckl", received, received, preferred_element_type=jnp.float32)


def per_device(activations, cotangent, sampled_rows, block_owner):
    tok_local = activations.shape[0]
    model_width = activations.shape[1]
    group_w = cotangent.shape[1]
    dp_count = lax.axis_size("dp")
    my_dp = lax.axis_index("dp")
    block_total = model_width // FACTOR_BLOCK
    capacity = max(1, block_total // dp_count)
    row_share = model_width // dp_count
    samples_all = S_DEV * dp_count
    grad_rows = lax.psum_scatter(
        lax.dot_general(
            activations, cotangent, (((0,), (0,)), ((), ())), preferred_element_type=jnp.float32
        ),
        "dp",
        scatter_dimension=0,
        tiled=True,
    )
    picked_acts = jnp.take(activations, sampled_rows, axis=0)
    picked_grads = jnp.take(cotangent, sampled_rows, axis=0)
    g_partial = lax.dot_general(
        picked_grads, picked_grads, (((0,), (0,)), ((), ())), preferred_element_type=jnp.float32
    )
    g_total = lax.psum(g_partial, "dp")
    g_factor = g_total * (tok_local / S_DEV) + DAMPING * jnp.eye(group_w, dtype=jnp.float32)
    slot_of = block_owner * capacity + block_rank(block_owner)
    dest_ids = jnp.arange(dp_count * capacity, dtype=jnp.int32)
    chooser = (slot_of[None, :] == dest_ids[:, None]).astype(jnp.bfloat16)
    row_blocks = picked_acts.reshape(S_DEV, block_total, FACTOR_BLOCK)
    outgoing = lax.dot_general(
        chooser, row_blocks, (((1,), (1,)), ((), ())), preferred_element_type=jnp.float32
    )
    outgoing = outgoing.astype(jnp.bfloat16).reshape(dp_count, capacity, S_DEV, FACTOR_BLOCK)
    gram_slots = owner_grams(
        lax.all_to_all(outgoing, "dp", split_axis=0, concat_axis=0, tiled=True)
    )
    a_factor = (
        gram_slots / samples_all + DAMPING * jnp.eye(FACTOR_BLOCK, dtype=jnp.float32)[None, :, :]
    )
    input_factor_inverse = newton_inverse(a_factor)
    owned_count = jnp.sum((block_owner == my_dp).astype(jnp.int32))
    slot_used = jnp.arange(capacity, dtype=jnp.int32) < owned_count
    owned_out = jnp.where(slot_used[:, None, None], input_factor_inverse, 0.0)
    g_inverse = newton_inverse(g_factor[None, :, :])[0]
    per_dev = max(1, row_share // FACTOR_BLOCK)
    rows_each = min(row_share, FACTOR_BLOCK)
    first_block = my_dp * row_share // FACTOR_BLOCK
    need_ids = first_block + jnp.arange(per_dev, dtype=jnp.int32)
    need_slots = jnp.take(slot_of, need_ids)
    row_offset = my_dp * row_share % FACTOR_BLOCK
    shard_piece = lax.all_gather(owned_out, "dp", axis=0, tiled=True)
    rows_part = lax.dynamic_slice_in_dim(shard_piece, row_offset, rows_each, 1)
    slot_ids = jnp.arange(shard_piece.shape[0], dtype=jnp.int32)
    selector = (need_slots[:, None] == slot_ids[None, :]).astype(jnp.float32)
    inverse_rows = jnp.einsum("jm,mkl->jkl", selector, rows_part, precision=precise_mode)
    grad_right = jnp.dot(
        grad_rows, g_inverse, precision=precise_mode, preferred_element_type=jnp.float32
    )
    partner = from_partner(grad_right, "dp", 0)
    is_lower = my_dp % 2 == 0
    joined = jnp.where(
        is_lower,
        jnp.concatenate([grad_right, partner], 0),
        jnp.concatenate([partner, grad_right], 0),
    )
    complete_rows = joined[None, :, :]
    natural_step = jnp.einsum("jrk,jkl->jrl", inverse_rows, complete_rows, precision=precise_mode)
    return (natural_step.reshape(row_share, group_w), owned_out)


def solution(mesh):
    return jax.shard_map(
        per_device,
        mesh=mesh,
        in_specs=(P("dp", None), P("dp", "tensor"), P("dp"), P()),
        out_specs=(P("dp", "tensor"), P("dp", None, None)),
        check_vma=False,
    )
```

profile of v0, /device:TPU:1, one launch (start us, length us, event | category | flops | bytes accessed | tf_op | source)
XLA Modules:
  0.0 975.9 jit_solution(2358637673614517384)
XLA Ops:
  7.2 0.7 compare_select_fusion
  7.9 0.7 compare_and_fusion
  8.6 0.7 gather_fusion.1
  9.3 1.0 fusion.37
  10.4 11.3 %fusion.52 = f32[8192,256]{1,0:T(8,128)} fusion(bf16[768,8192]{1,0:T(8,128)(2,1)} %param.8, bf16[768,256]{1,0:T(8,128)(2,1)S(1)} %copy-done), kind=kOutput, calls=%fused_computation.68 | convolution fusion | flops 3221225472 | bytes 21364736 | tf_op jit(solution)/shard_map/dot_general | solution.py:61
  21.7 8.4 gather_fusion
  30.5 0.6 fusion.47
  31.4 0.8 convert_bitcast_fusion
  32.2 2.5 copy.21
  34.7 10.3 %all-to-all-start = ((bf16[64,1,64,256]{3,2,1,0:T(8,128)(2,1)}), bf16[64,1,64,256]{3,2,1,0:T(8,128)(2,1)S(1)}, u32[]{:S(2)}, u32[]{:S(2)}) async-start(bf16[64,1,64,256]{3,2,1,0:T(8,128)(2,1)} %copy.21), calls=%async_computation | async-start | bytes 4194304 | tf_op jit(solution)/shard_map/all_to_all | solution.py:84
  45.9 29.0 %all-to-all-done = bf16[64,1,64,256]{3,2,1,0:T(8,128)(2,1)S(1)} async-done(((bf16[64,1,64,256]{3,2,1,0:T(8,128)(2,1)}), bf16[64,1,64,256]{3,2,1,0:T(8,128)(2,1)S(1)}, u32[]{:S(2)}, u32[]{:S(2)}) %all-to-all-start) | async-done | bytes 2097184 | tf_op jit(solution)/shard_map/all_to_all | solution.py:84
  74.9 0.9 abs_reduce_fusion.1
  75.9 0.7 reduce_max.18
  77.6 10.7 %while.23 = (s32[]{:T(128)}, f32[1,256,256]{1,2,0:T(8,128)S(1)}, f32[1,256,256]{2,1,0:T(8,128)S(1)}, s32[]{:T(128)}) while((s32[]{:T(128)}, f32[1,256,256]{1,2,0:T(8,128)S(1)}, f32[1,256,256]{2,1,0:T(8,128)S(1)}, s32[]{:T(128)}) %tuple.58), condition=%wide.region_5.6_spmd.clone, body=%wide.region_4.5_spmd.clone.sunk | while | flops 402849792 | bytes 2097205 | solution.py:35
  78.0 0.6 convolution_bitcast_fusion.4
  79.1 0.6 convolution_bitcast_fusion.4
  80.2 0.6 convolution_bitcast_fusion.4
  81.2 0.6 convolution_bitcast_fusion.4
  82.3 0.6 convolution_bitcast_fusion.4
  83.4 0.6 convolution_bitcast_fusion.4
  84.5 0.6 convolution_bitcast_fusion.4
  85.1 0.4 convolution_subtract_fusion.4
  85.5 0.6 convolution_bitcast_fusion.4
  86.6 0.6 convolution_bitcast_fusion.4
  87.7 0.6 convolution_bitcast_fusion.4
  88.4 0.7 broadcast_select_fusion
  89.2 0.7 dynamic-slice.2
  90.5 438.1 %all-reduce.2.cloned.1.call-done = f32[256,256]{0,1:T(8,128)} async-done(((f32[256,256]{0,1:T(8,128)}), f32[256,256]{0,1:T(8,128)}) %all-reduce.2.cloned.1.call-update) | async-done | bytes 262160 | tf_op jit(solution)/shard_map/psum | solution.py:73
  528.6 1.0 fusion.33
  529.6 0.6 reduce_max.19
  531.1 10.7 %while.24 = (s32[]{:T(128)}, f32[1,256,256]{1,2,0:T(8,128)S(1)}, f32[1,256,256]{2,1,0:T(8,128)S(1)}, s32[]{:T(128)}) while((s32[]{:T(128)}, f32[1,256,256]{1,2,0:T(8,128)S(1)}, f32[1,256,256]{2,1,0:T(8,128)S(1)}, s32[]{:T(128)}) %tuple.55), condition=%wide.region_11.12_spmd.clone, body=%wide.region_10.11_spmd.clone.sunk | while | flops 402849792 | bytes 2097205 | solution.py:35
  531.6 0.6 convolution_bitcast_fusion.5
  532.6 0.6 convolution_bitcast_fusion.5
  533.7 0.6 convolution_bitcast_fusion.5
  534.8 0.6 convolution_bitcast_fusion.5
  535.8 0.6 convolution_bitcast_fusion.5
  536.9 0.6 convolution_bitcast_fusion.5
  538.0 0.6 convolution_bitcast_fusion.5
  539.1 0.6 convolution_bitcast_fusion.5
  540.1 0.6 convolution_bitcast_fusion.5
  541.2 0.6 convolution_bitcast_fusion.5
  541.8 286.0 %reduce-scatter.2.cloned.1.call-done = f32[128,256]{1,0:T(8,128)} async-done(((f32[8192,256]{1,0:T(8,128)}), f32[128,256]{1,0:T(8,128)}) %reduce-scatter.2.cloned.1.call-update) | async-done | bytes 131088 | tf_op jit(solution)/shard_map/reduce_scatter | solution.py:60
  827.8 1.3 fusion.29
  829.1 6.3 collective-permute-start
  835.4 121.7 %all-gather.2.cloned.1.call-done = f32[64,256,256]{2,1,0:T(8,128)} async-done(((f32[1,256,256]{2,1,0:T(8,128)}), f32[64,256,256]{2,1,0:T(8,128)}) %all-gather.2.cloned.1.call-update) | async-done | bytes 16777232 | tf_op jit(solution)/shard_map/all_gather | solution.py:100
  957.0 3.9 constant_dynamic-slice_fusion
  961.0 7.5 fusion.10
  968.5 0.9 fusion.23
  (61 shorter events, 10.0 us)
Async XLA Ops:
  7.2 1.4 copy-start
  7.2 521.4 %all-reduce.2.cloned.1.call-start = ((), (), s32[]{:S(2)}) async-start(), calls=%async_computation.4 | async-start | bytes 524288 | tf_op jit(solution)/shard_map/psum | solution.py:73
  10.3 817.5 %reduce-scatter.2.cloned.1.call-start = ((), (), s32[]{:S(2)}) async-start(), calls=%async_computation.3 | async-start | bytes 8519680 | tf_op jit(solution)/shard_map/reduce_scatter | solution.py:60
  21.7 8.7 copy-start.1
  34.7 40.2 %all-to-all-start = ((bf16[64,1,64,256]{3,2,1,0:T(8,128)(2,1)}), bf16[64,1,64,256]{3,2,1,0:T(8,128)(2,1)S(1)}, u32[]{:S(2)}, u32[]{:S(2)}) async-start(bf16[64,1,64,256]{3,2,1,0:T(8,128)(2,1)} %copy.21), calls=%async_computation | async-start | bytes 4194304 | tf_op jit(solution)/shard_map/all_to_all | solution.py:84
  45.1 912.0 %all-gather.2.cloned.1.call-start = ((), (), s32[]{:S(2)}) async-start(), calls=%async_computation.2 | async-start | bytes 17039360 | tf_op jit(solution)/shard_map/all_gather | solution.py:100
  829.1 139.4 %collective-permute-start = (f32[128,256]{1,0:T(8,128)S(1)}, f32[128,256]{1,0:T(8,128)S(1)}, u32[]{:S(2)}, u32[]{:S(2)}) collective-permute-start(f32[128,256]{1,0:T(8,128)S(1)} %fusion.29), channel_id=1, source_target_pairs={{0,4},{4,0},{8,12},{12,8},{16,20},{20,16},{24,28},{28,24},{32,36},... | collective-permute-start | bytes 393224 | tf_op jit(solution)/shard_map/ppermute | solution.py:20
Sparse Core Ops, SparseCore 0:
  10.6 517.9 all-reduce.1
  531.1 296.6 reduce-scatter.1
  830.2 126.7 all-gather.1
where the time goes:
time: 976 us
  waiting for transfers between devices  875 us (90%)
  matrix products  44 us (5%)
  local copies, waits for them, and re-layouts  17.5 us (2%)
  starting transfers between devices  16.9 us (2%)
  between operations  16.6 us (2%)
    psum x1, waiting for transfers between devices, per_device(): g_total = lax.psum(g_partial, 'dp')  438 us
    reduce_scatter x1, waiting for transfers between devices, per_device(): lax.psum_scatter(lax.dot_general(activations, cotangent, (((0,), (0,)), (...  286 us
    all_gather x1, waiting for transfers between devices, per_device(): shard_piece = lax.all_gather(owned_out, 'dp', axis=0, tiled=True)  122 us
    all_to_all x1, waiting for transfers between devices, per_device(): lax.all_to_all(outgoing, 'dp', split_axis=0, concat_axis=0, tiled=True)  29 us
  transfers between devices with their start and end apart: 5, of which 4 were waited for; matrix products, arithmetic and copies ran while one was open for 6% of the time, Pallas kernels for 0%

commit v1 on v0

--- a/solution.py
+++ b/solution.py
@@ -70,7 +70,7 @@
     g_partial = lax.dot_general(
         picked_grads, picked_grads, (((0,), (0,)), ((), ())), preferred_element_type=jnp.float32
     )
-    g_total = lax.psum(g_partial, "dp")
+    g_total = jnp.sum(lax.all_gather(g_partial, "dp"), axis=0)
     g_factor = g_total * (tok_local / S_DEV) + DAMPING * jnp.eye(group_w, dtype=jnp.float32)
     slot_of = block_owner * capacity + block_rank(block_owner)
     dest_ids = jnp.arange(dp_count * capacity, dtype=jnp.int32)

time: 976 us -> 609 us (0.62)
  waiting for transfers between devices: 875 us -> 502 us
    psum x1 -> x0, waiting for transfers between devices: 438 us -> none  [per_device(): g_total = lax.psum(g_partial, 'dp')]
    all_gather x0 -> x1, waiting for transfers between devices: none -> 64.3 us  [per_device(): g_total = jnp.sum(lax.all_gather(g_partial, 'dp'), axis=0)]
  transfers between devices with their start and end apart: 5 -> 5, of which waited for: 4 -> 4; matrix products, arithmetic and copies ran while one was open for 6% -> 11% of each run, Pallas kernels for 0% -> 0%
where the time goes in v1:
time: 609 us
  waiting for transfers between devices  502 us (82%)
  matrix products  44 us (7%)
  local copies, waits for them, and re-layouts  18.1 us (3%)
  starting transfers between devices  16.4 us (3%)
  between operations  16.4 us (3%)
  other arithmetic  10.6 us (2%)
    reduce_scatter x1, waiting for transfers between devices, per_device(): lax.psum_scatter(lax.dot_general(activations, cotangent, (((0,), (0,)), (...  282 us
    all_gather x1, waiting for transfers between devices, per_device(): shard_piece = lax.all_gather(owned_out, 'dp', axis=0, tiled=True)  121 us
    all_gather x1, waiting for transfers between devices, per_device(): g_total = jnp.sum(lax.all_gather(g_partial, 'dp'), axis=0)  64.3 us
    all_to_all x1, waiting for transfers between devices, per_device(): lax.all_to_all(outgoing, 'dp', split_axis=0, concat_axis=0, tiled=True)  34.8 us
  transfers between devices with their start and end apart: 5, of which 4 were waited for; matrix products, arithmetic and copies ran while one was open for 11% of the time, Pallas kernels for 0%

profile of v1, /device:TPU:1, one launch (start us, length us, event | category | flops | bytes accessed | tf_op | source)
XLA Modules:
  0.0 608.7 jit_solution(12871172747344295638)
XLA Ops:
  7.2 0.7 compare_select_fusion
  7.9 0.7 compare_and_fusion
  8.6 0.7 gather_fusion.1
  9.3 1.0 fusion.38
  10.4 11.3 %fusion.53 = f32[8192,256]{1,0:T(8,128)} fusion(bf16[768,8192]{1,0:T(8,128)(2,1)} %param.8, bf16[768,256]{1,0:T(8,128)(2,1)S(1)} %copy-done), kind=kOutput, calls=%fused_computation.69 | convolution fusion | flops 3221225472 | bytes 21364736 | tf_op jit(solution)/shard_map/dot_general | solution.py:61
  21.7 8.3 %gather_fusion = bf16[64,8192]{1,0:T(8,128)(2,1)S(1)} fusion(bf16[768,8192]{1,0:T(8,128)(2,1)} %param.8, s32[1024]{0:T(1024)S(1)} %pad_clamp_fusion), kind=kCustom, calls=%fused_computation | custom fusion | bytes 2097408 | tf_op jit(solution)/shard_map/jit(_take)/gather | solution.py:68
  30.5 0.7 fusion.48
  31.4 0.8 convert_bitcast_fusion
  32.2 2.5 copy.17
  34.7 10.5 %all-to-all-start = ((bf16[64,1,64,256]{3,2,1,0:T(8,128)(2,1)}), bf16[64,1,64,256]{3,2,1,0:T(8,128)(2,1)S(1)}, u32[]{:S(2)}, u32[]{:S(2)}) async-start(bf16[64,1,64,256]{3,2,1,0:T(8,128)(2,1)} %copy.17), calls=%async_computation | async-start | bytes 4194304 | tf_op jit(solution)/shard_map/all_to_all | solution.py:84
  46.1 34.8 %all-to-all-done = bf16[64,1,64,256]{3,2,1,0:T(8,128)(2,1)S(1)} async-done(((bf16[64,1,64,256]{3,2,1,0:T(8,128)(2,1)}), bf16[64,1,64,256]{3,2,1,0:T(8,128)(2,1)S(1)}, u32[]{:S(2)}, u32[]{:S(2)}) %all-to-all-start) | async-done | bytes 2097184 | tf_op jit(solution)/shard_map/all_to_all | solution.py:84
  80.9 0.9 abs_reduce_fusion
  81.9 0.6 reduce_max.18
  83.2 10.7 %while.23 = (s32[]{:T(128)}, f32[1,256,256]{1,2,0:T(8,128)S(1)}, f32[1,256,256]{2,1,0:T(8,128)S(1)}, s32[]{:T(128)}) while((s32[]{:T(128)}, f32[1,256,256]{1,2,0:T(8,128)S(1)}, f32[1,256,256]{2,1,0:T(8,128)S(1)}, s32[]{:T(128)}) %tuple.60), condition=%wide.region_5.6_spmd.clone, body=%wide.region_4.5_spmd.clone.sunk | while | flops 402849792 | bytes 2097205 | solution.py:35
  83.6 0.6 convolution_bitcast_fusion.4
  84.7 0.6 convolution_bitcast_fusion.4
  85.8 0.6 convolution_bitcast_fusion.4
  86.8 0.6 convolution_bitcast_fusion.4
  87.9 0.6 convolution_bitcast_fusion.4
  89.0 0.6 convolution_bitcast_fusion.4
  90.1 0.6 convolution_bitcast_fusion.4
  90.7 0.4 convolution_subtract_fusion.4
  91.1 0.6 convolution_bitcast_fusion.4
  92.2 0.6 convolution_bitcast_fusion.4
  93.3 0.6 convolution_bitcast_fusion.4
  93.9 0.8 copy.19
  94.8 0.6 dynamic-slice.2
  96.0 64.3 %all-gather.6.cloned.1.call-done = f32[16384,256]{1,0:T(8,128)} async-done(((f32[256,256]{1,0:T(8,128)}), f32[16384,256]{1,0:T(8,128)}) %all-gather.6.cloned.1.call-update) | async-done | bytes 16777232 | tf_op jit(solution)/shard_map/all_gather | solution.py:73
  160.3 6.8 %reduce_sum.48 = f32[256,256]{1,0:T(8,128)S(1)} reduce(f32[64,256,256]{2,1,0:T(8,128)} %bitcast.91, f32[]{:T(128)} %constant.116.clone.1), dimensions={0}, to_apply=%region_7.8 | reduce | flops 4128768 | bytes 17039364 | tf_op jit(solution)/shard_map/reduce_sum | solution.py:73
  167.6 0.6 reduce_max.19
  168.9 10.7 %while.24 = (s32[]{:T(128)}, f32[1,256,256]{1,2,0:T(8,128)S(1)}, f32[1,256,256]{2,1,0:T(8,128)S(1)}, s32[]{:T(128)}) while((s32[]{:T(128)}, f32[1,256,256]{1,2,0:T(8,128)S(1)}, f32[1,256,256]{2,1,0:T(8,128)S(1)}, s32[]{:T(128)}) %tuple.57), condition=%wide.region_11.12_spmd.clone, body=%wide.region_10.11_spmd.clone.sunk | while | flops 402849792 | bytes 2097205 | solution.py:35
  169.3 0.6 convolution_bitcast_fusion.5
  170.4 0.6 convolution_bitcast_fusion.5
  171.4 0.6 convolution_bitcast_fusion.5
  172.5 0.6 convolution_bitcast_fusion.5
  173.6 0.6 convolution_bitcast_fusion.5
  174.7 0.6 convolution_bitcast_fusion.5
  175.7 0.6 convolution_bitcast_fusion.5
  176.8 0.6 convolution_bitcast_fusion.5
  177.9 0.6 convolution_bitcast_fusion.5
  178.9 0.6 convolution_bitcast_fusion.5
  179.6 281.9 %reduce-scatter.2.cloned.1.call-done = f32[128,256]{1,0:T(8,128)} async-done(((f32[8192,256]{1,0:T(8,128)}), f32[128,256]{1,0:T(8,128)}) %reduce-scatter.2.cloned.1.call-update) | async-done | bytes 131088 | tf_op jit(solution)/shard_map/reduce_scatter | solution.py:60
  461.5 1.3 fusion.31
  462.8 5.6 collective-permute-start
  468.4 121.4 %all-gather.4.cloned.1.call-done = f32[64,256,256]{2,1,0:T(8,128)} async-done(((f32[1,256,256]{2,1,0:T(8,128)}), f32[64,256,256]{2,1,0:T(8,128)}) %all-gather.4.cloned.1.call-update) | async-done | bytes 16777232 | tf_op jit(solution)/shard_map/all_gather | solution.py:100
  589.7 4.0 constant_dynamic-slice_fusion
  593.7 7.5 %fusion.10 = f32[1,128,256]{2,0,1:T(1,128)S(1)} fusion(f32[64,128,256]{2,1,0:T(8,128)S(1)} %constant_dynamic-slice_fusion, s32[]{:T(128)} %bitcast.2), kind=kOutput, calls=%fused_computation.16 | convolution fusion | flops 25165888 | bytes 8519684 | tf_op jit(solution)/shard_map/jm,mkl->jkl/dot_general | solution.py:104
  601.2 0.9 fusion.25
  (64 shorter events, 9.8 us)
Async XLA Ops:
  7.2 1.4 copy-start
  7.2 153.2 %all-gather.6.cloned.1.call-start = ((), (), s32[]{:S(2)}) async-start(), calls=%async_computation.4 | async-start | bytes 17039360 | tf_op jit(solution)/shard_map/all_gather | solution.py:73
  10.3 451.2 %reduce-scatter.2.cloned.1.call-start = ((), (), s32[]{:S(2)}) async-start(), calls=%async_computation.3 | async-start | bytes 8519680 | tf_op jit(solution)/shard_map/reduce_scatter | solution.py:60
  21.6 8.7 %copy-start.2 = (s32[32]{0:T(128)S(1)}, s32[32]{0:T(128)}, u32[]{:S(2)}) copy-start(s32[32]{0:T(128)} %param.11) | copy-start | bytes 388
  34.7 46.1 %all-to-all-start = ((bf16[64,1,64,256]{3,2,1,0:T(8,128)(2,1)}), bf16[64,1,64,256]{3,2,1,0:T(8,128)(2,1)S(1)}, u32[]{:S(2)}, u32[]{:S(2)}) async-start(bf16[64,1,64,256]{3,2,1,0:T(8,128)(2,1)} %copy.17), calls=%async_computation | async-start | bytes 4194304 | tf_op jit(solution)/shard_map/all_to_all | solution.py:84
  45.2 544.5 %all-gather.4.cloned.1.call-start = ((), (), s32[]{:S(2)}) async-start(), calls=%async_computation.2 | async-start | bytes 17039360 | tf_op jit(solution)/shard_map/all_gather | solution.py:100
  462.8 138.4 %collective-permute-start = (f32[128,256]{1,0:T(8,128)S(1)}, f32[128,256]{1,0:T(8,128)S(1)}, u32[]{:S(2)}, u32[]{:S(2)}) collective-permute-start(f32[128,256]{1,0:T(8,128)S(1)} %fusion.31), channel_id=1, source_target_pairs={{0,4},{4,0},{8,12},{12,8},{16,20},{20,16},{24,28},{28,24},{32,36},... | collective-permute-start | bytes 393224 | tf_op jit(solution)/shard_map/ppermute | solution.py:20
  589.7 12.4 %copy-start.1 = (bf16[768,256]{1,0:T(8,128)(2,1)S(1)}, bf16[768,256]{1,0:T(8,128)(2,1)}, u32[]{:S(2)}) copy-start(bf16[768,256]{1,0:T(8,128)(2,1)} %param.9) | copy-start | bytes 1179652
Sparse Core Ops, SparseCore 0:
  10.4 149.8 all-gather.5
  162.9 298.5 reduce-scatter.1
  463.9 125.7 all-gather.3
